TPU v7x, 32 devices: a whole 2x2x4 slice. The times are simulated.
32 devices in a mesh: row: 4 (over z), col: 8 (over y, x, core).
Axes of the slice: x: 2, y: 2, z: 4, core: 2. Of those that a mesh axis runs over, the one named last changes fastest.
Arguments:
- activations: bfloat16 [4096, 4096], P('col', 'row'), may hold values from -6 to 6
- out_grads: bfloat16 [4096, 2048], P('row', 'col'), may hold values from -0.09375 to 0.09375
- statistics: float32 [4, 8, 512, 1024], P('row', 'col'), may hold values from -10 to 200, as said below
Outputs:
- new_statistics: float32 [4, 8, 512, 1024], P('row', 'col')
- update: bfloat16 [4096, 2048], P('row', 'col')
Inputs may be any that keep to these rules, and one draw needn't show every extreme that they name: `statistics`: every statistic is symmetric and positive definite.
All inputs are finite; a program needn't handle non-finite values.
Results may differ from a plain program's by a relative error of at most 0.0017.
The roundings to bfloat16 on the way count: a program that leaves them out, or rounds other values in their place, can miss the bound.
Values may be sent and summed in bfloat16 or wider, within the bound.
A program may use at most 128 MiB of HBM per device.

v0:
```python
import functools

import jax
import jax.numpy as jnp
from jax import lax
from jax.experimental import pallas as pl
from jax.experimental.pallas import tpu as pltpu
from jax.sharding import PartitionSpec as P

DAMP_EXP = 3
DECAY = 0.9
EPS = 1e-06

F32 = jnp.float32
BF16 = jnp.bfloat16


def product(left, right, over=((1,), (0,))):
    return lax.dot_general(left, right, (over, ((), ())), preferred_element_type=F32)


def split(value):
    high = value.astype(BF16)
    return high, (value - high.astype(F32)).astype(BF16)


def total(value):
    return jnp.sum(jnp.sum(value, axis=1, keepdims=True), axis=0, keepdims=True)


def flip(index, bit):
    return index + (1 - 2 * (index // (1 << bit) % 2)) * (1 << bit)


def shampoo_kernel(
    rows,
    cols,
    act,
    og,
    stat,
    renewed,
    update,
    acts,
    grads,
    partial,
    from_sibling,
    pair_own,
    pair_other,
    other_diag,
    f_hi,
    f_lo,
    q_hi,
    q_lo,
    w_hi,
    w_lo,
    p_hi,
    p_lo,
    root,
    root_sibling,
    left,
    left_other,
    hp,
    send_sem,
    recv_sem,
    local_sem,
):
    row = lax.axis_index("row")
    col = lax.axis_index("col")
    side = col % 2
    half_index = col // 2 % 2
    half, order = stat.shape
    piece = act.shape[0]
    width = og.shape[1]
    pieces = cols // 2
    bits = pieces.bit_length() - 1
    block = min(256, half)
    used = [0]

    def at_col(bit):
        return (row, flip(col, bit))

    def send(src, dst, device):
        slot = used[0]
        used[0] += 1
        copy = pltpu.make_async_remote_copy(
            src_ref=src,
            dst_ref=dst,
            send_sem=send_sem.at[slot],
            recv_sem=recv_sem.at[slot],
            device_id=device,
            device_id_type=pl.DeviceIdType.MESH,
        )
        copy.start()
        return copy

    def piece_ref(index):
        return act if index == 0 else acts.at[index - 1]

    def lanes(index, size):
        return pl.ds(pl.multiple_of(index * size, size), size)

    barrier = pltpu.get_barrier_semaphore()
    friends = [at_col(bit) for bit in range(bits + 1)]
    friends += [((row + step) % rows, col) for step in range(1, rows)]
    for friend in friends:
        pl.semaphore_signal(
            barrier, inc=1, device_id=friend, device_id_type=pl.DeviceIdType.MESH
        )
    pl.semaphore_wait(barrier, len(friends))

    arrivals = {}

    def forward(index):
        for bit in range(1, bits + 1):
            if 1 << (bit - 1) > index:
                slot = (1 << (bit - 1)) + index
                arrivals[slot] = send(piece_ref(index), acts.at[slot - 1], at_col(bit))

    own_columns = lanes(side, width)
    sibling_og = send(
        og.at[lanes(1 - side, piece)], grads.at[row, :, own_columns], at_col(0)
    )
    kept = pltpu.make_async_copy(
        og.at[lanes(side, piece)], grads.at[row, :, own_columns], local_sem.at[0]
    )
    kept.start()
    forward(0)
    diag_copy = send(stat.at[:, lanes(half_index, half)], other_diag, at_col(1))
    kept.wait()
    sibling_og.wait()
    og_copies = [
        send(grads.at[row], grads.at[row], ((row + step) % rows, col)) for step in range(1, rows)
    ]

    own_max = jnp.max(
        jnp.sum(jnp.abs(stat[...]), axis=1, keepdims=True), axis=0, keepdims=True
    )
    eye = (
        lax.broadcasted_iota(jnp.int32, (half, half), 0)
        == lax.broadcasted_iota(jnp.int32, (half, half), 1)
    ).astype(F32)
    own_trace = total(stat[:, lanes(half_index, half)] * eye)

    def add_piece(index):
        source = col // 2
        for bit in range(bits):
            if index >> bit & 1:
                source = flip(source, bit)

        def rows_of(step, carry):
            here = lanes(step, block)
            term = product(piece_ref(index)[:, here], grads[source], ((0,), (0,)))
            if index == 0:
                partial[here, :] = term
            else:
                partial[here, :] += term
            return carry

        lax.fori_loop(0, order // block, rows_of, 0)

    for index in range(1, pieces):
        arrivals[index].wait_recv()
        forward(index)
    for copy in og_copies:
        copy.wait_recv()
    for index in range(pieces):
        add_piece(index)
    swap = send(partial.at[:, lanes(1 - side, width)], from_sibling, at_col(0))

    diag_copy.wait_recv()
    own_off = stat[:, lanes(1 - half_index, half)]
    far = other_diag[...]
    far_sums = jnp.sum(jnp.abs(own_off), axis=0, keepdims=True) + jnp.sum(
        jnp.abs(far), axis=0, keepdims=True
    )
    far_max = jnp.max(far_sums, axis=1, keepdims=True)
    damping = 10.0 ** (-DAMP_EXP) * (own_trace + total(far * eye)) / order
    scaling = (jnp.maximum(own_max, far_max) + damping) / 4.0
    scale = 0.25 / scaling
    shift = 1.25 - damping * scale
    top = shift * eye - stat[:, lanes(half_index, half)] * scale
    f_hi[:half, :half], f_lo[:half, :half] = split(top)
    off = -(own_off * scale)
    f_hi[:half, half:], f_lo[:half, half:] = split(off)
    f_hi[half:, :half], f_lo[half:, :half] = split(off.T)
    f_hi[half:, half:], f_lo[half:, half:] = split(shift * eye - far * scale)

    def triple(a_hi, a_lo, b_hi, b_lo, here):
        return (
            product(a_hi[here, :], b_hi[...])
            + product(a_hi[here, :], b_lo[...])
            + product(a_lo[here, :], b_hi[...])
        )

    def square_rows(step, carry):
        here = lanes(step, block)
        square = triple(f_hi, f_lo, f_hi, f_lo, here)
        q_hi[here, :], q_lo[here, :] = split(square)
        rest = 5.0 * (f_hi[here, :].astype(F32) + f_lo[here, :].astype(F32)) - 4.0 * square
        w_hi[here, :], w_lo[here, :] = split(rest)
        return carry

    lax.fori_loop(0, order // block, square_rows, 0)

    swap.wait_recv()
    tile = (partial[:, own_columns] + from_sibling[...]).astype(BF16)
    pair_own[:, own_columns] = tile
    tile_sibling = send(pair_own.at[:, own_columns], pair_own.at[:, own_columns], at_col(0))
    tile_far = send(pair_own.at[:, own_columns], pair_other.at[:, own_columns], at_col(1))

    def fourth_rows(step, carry):
        here = lanes(step, block)
        p_hi[here, :], p_lo[here, :] = split(triple(q_hi, q_lo, q_hi, q_lo, here))
        return carry

    lax.fori_loop(0, half // block, fourth_rows, 0)

    def root_rows(step, carry):
        here = lanes(step, block)
        value = 5.0 * (f_hi[here, :].astype(F32) + f_lo[here, :].astype(F32))
        value = (value - triple(p_hi, p_lo, w_hi, w_lo, here)) / 4.0
        root[here, :] = value.astype(BF16)
        return carry

    lax.fori_loop(0, half // block, root_rows, 0)
    root_copy = send(root, root_sibling, at_col(0))
    tile_far.wait_recv()
    far_sibling = send(pair_other.at[:, own_columns], pair_other.at[:, own_columns], at_col(0))
    root_copy.wait_recv()
    left[...] = jnp.where(side == 0, root[...], root_sibling[...])
    left_copy = send(left.at[:, pl.ds(0, half)], left_other, at_col(1))
    tile_sibling.wait_recv()
    far_sibling.wait_recv()

    fresh = (1.0 - DECAY) / order

    @pl.when(side == 0)
    def _():
        def gram_rows(step, carry):
            there = pl.ds(pl.multiple_of(half_index * half + step * block, block), block)
            here = lanes(step, block)
            gram = product(pair_own[there, :], pair_own[...], ((1,), (1,)))
            gram += product(pair_other[there, :], pair_other[...], ((1,), (1,)))
            renewed[here, :] = DECAY * stat[here, :] + fresh * gram
            return carry

        lax.fori_loop(0, half // block, gram_rows, 0)

    @pl.when(side == 1)
    def _():
        def gram_rows(step, carry):
            here = lanes(step, block)
            mine = pair_own[:, here]
            for position, pair in ((half_index, pair_own), (1 - half_index, pair_other)):
                there = lanes(position, half)
                gram = product(mine, pair[...], ((0,), (0,)))
                renewed[here, there] = DECAY * stat[here, there] + fresh * gram
            return carry

        lax.fori_loop(0, half // block, gram_rows, 0)

    right = jnp.where(side == 0, root_sibling[:width, :], root[half - width :, :])
    for place, natural in ((0, half_index), (1, 1 - half_index)):
        there = lanes(natural, half)
        value = product(pair_own[there, :], right[:, :half], ((1,), (1,)))
        value += product(pair_other[there, :], right[:, half:], ((1,), (1,)))
        hp[place * half : (place + 1) * half, :] = value.astype(BF16)
    cond_own = product(left[...], hp[...])
    cond_other = product(left[:, half:], hp[:half, :], ((0,), (0,)))
    left_copy.wait_recv()
    cond_other += product(left_other[...], hp[half:, :])
    values = pair_own[:, own_columns].astype(F32)
    count = order * width
    power = (total(cond_own * cond_own) + total(cond_other * cond_other)) / count
    ratio = jnp.sqrt(total(values * values) / count / (power + EPS))
    update[lanes(half_index, half), :] = (cond_own * ratio).astype(BF16)
    update[lanes(1 - half_index, half), :] = (cond_other * ratio).astype(BF16)

    everything = [list(arrivals.values()), og_copies]
    everything += [[diag_copy, swap, tile_sibling, tile_far, root_copy, far_sibling, left_copy]]
    for group in everything:
        for copy in group:
            copy.wait_send()


def local(rows, cols, activations, out_grads, statistics):
    stat = statistics[0, 0]
    half, order = stat.shape
    piece = activations.shape[0]
    width = out_grads.shape[1]
    pieces = cols // 2
    copies = pieces - 1 + rows - 1 + 8
    square = pltpu.VMEM((order, order), BF16)
    strip = pltpu.VMEM((half, order), BF16)
    pair = pltpu.VMEM((order, 2 * width), BF16)
    renewed, update = pl.pallas_call(
        functools.partial(shampoo_kernel, rows, cols),
        out_shape=(
            jax.ShapeDtypeStruct((half, order), F32),
            jax.ShapeDtypeStruct((order, width), BF16),
        ),
        in_specs=[pl.BlockSpec(memory_space=pltpu.VMEM)] * 3,
        out_specs=[pl.BlockSpec(memory_space=pltpu.VMEM)] * 2,
        scratch_shapes=[
            pltpu.VMEM((pieces - 1, piece, order), BF16),
            pltpu.VMEM((rows, piece, 2 * width), BF16),
            pltpu.VMEM((order, 2 * width), F32),
            pltpu.VMEM((order, width), F32),
            pair,
            pair,
            pltpu.VMEM((half, half), F32),
            square,
            square,
            square,
            square,
            square,
            square,
            strip,
            strip,
            strip,
            strip,
            strip,
            pltpu.VMEM((half, half), BF16),
            pltpu.VMEM((order, width), BF16),
            pltpu.SemaphoreType.DMA((copies,)),
            pltpu.SemaphoreType.DMA((copies,)),
            pltpu.SemaphoreType.DMA((1,)),
        ],
        compiler_params=pltpu.CompilerParams(
            collective_id=0, has_side_effects=True, vmem_limit_bytes=60 * 1024 * 1024
        ),
    )(activations, out_grads, stat)
    return (renewed[None, None], update)


def solution(mesh):
    placed = (P("col", "row"), P("row", "col"), P("row", "col", None, None))
    return jax.shard_map(
        functools.partial(local, mesh.shape["row"], mesh.shape["col"]),
        mesh=mesh,
        in_specs=placed,
        out_specs=(P("row", "col", None, None), P("row", "col")),
        check_vma=False,
    )
```

profile of v0, /device:TPU:0, one launch (start us, length us, event | category | flops | bytes accessed | tf_op | source)
XLA Modules:
  0.0 100.1 jit_solution(11459597956619674486)
XLA Ops:
  0.6 95.4 %shard_map.50 = (f32[512,1024]{1,0:T(8,128)}, bf16[1024,256]{1,0:T(8,128)(2,1)}) custom-call(bf16[512,1024]{1,0:T(8,128)(2,1)} %act.1, bf16[1024,256]{1,0:T(8,128)(2,1)} %og.1, f32[512,1024]{1,0:T(8,128)} %bitcast.2), custom_call_target="tpu_custom_call" | custom-call | tf_op jit(solution)/shard_map/pallas_call | solution.py:296
  96.1 0.0 copy-start
  96.1 3.2 %copy.7 = f32[1,1,512,1024]{3,2,1,0:T(8,128)} copy(f32[1,1,512,1024]{3,2,1,0:T(8,128)} %bitcast.3) | data formatting | bytes 4194304
  99.3 0.0 copy-done
  99.3 0.8 copy.8
Async XLA Ops:
  96.1 3.2 %copy-start = (bf16[1024,256]{1,0:T(8,128)(2,1)S(1)}, bf16[1024,256]{1,0:T(8,128)(2,1)}, u32[]{:S(2)}) copy-start(bf16[1024,256]{1,0:T(8,128)(2,1)} %get-tuple-element.9) | copy-start | bytes 1572868
where the time goes:
time: 101 us; the launch traced here: 100 us
  Pallas kernels  95.4 us (94%)
  local copies, waits for them, and re-layouts  4.01 us (4%)
    pallas_call x1, Pallas kernels, local(): pl.pallas_call(functools.partial(shampoo_kernel, rows, cols), out_shape=(...  95.4 us
    unnamed x4, local copies, waits for them, and re-layouts  4.01 us

commit v1 on v0

--- a/solution.py
+++ b/solution.py
@@ -73,16 +73,16 @@
     width = og.shape[1]
     pieces = cols // 2
     bits = pieces.bit_length() - 1
-    block = min(256, half)
+    block = width
     used = [0]
 
     def at_col(bit):
         return (row, flip(col, bit))
 
-    def send(src, dst, device):
+    def remote(src, dst, device):
         slot = used[0]
         used[0] += 1
-        copy = pltpu.make_async_remote_copy(
+        return pltpu.make_async_remote_copy(
             src_ref=src,
             dst_ref=dst,
             send_sem=send_sem.at[slot],
@@ -90,6 +90,9 @@
             device_id=device,
             device_id_type=pl.DeviceIdType.MESH,
         )
+
+    def send(src, dst, device):
+        copy = remote(src, dst, device)
         copy.start()
         return copy
 
@@ -128,9 +131,30 @@
     diag_copy = send(stat.at[:, lanes(half_index, half)], other_diag, at_col(1))
     kept.wait()
     sibling_og.wait()
-    og_copies = [
-        send(grads.at[row], grads.at[row], ((row + step) % rows, col)) for step in range(1, rows)
-    ]
+
+    hops = []
+    for hop in range(rows - 1):
+        for sign in (1, -1):
+            source = (row - sign * hop + rows) % rows
+            target = (row + sign + rows) % rows
+            copy = remote(grads.at[source], grads.at[source], (target, col))
+            last = rows - 1 if sign == 1 else 0
+            has_source = row - hop >= 0 if sign == 1 else row + hop < rows
+            sends = jnp.logical_and(has_source, row != last)
+            gets = row - 1 - hop >= 0 if sign == 1 else row + 1 + hop < rows
+            hops.append((hop, copy, sends, gets))
+
+    def start_hop(hop):
+        for number, copy, sends, _ in hops:
+            if number == hop:
+                pl.when(sends)(copy.start)
+
+    def wait_hop(hop):
+        for number, copy, _, gets in hops:
+            if number == hop:
+                pl.when(gets)(copy.wait_recv)
+
+    start_hop(0)
 
     own_max = jnp.max(
         jnp.sum(jnp.abs(stat[...]), axis=1, keepdims=True), axis=0, keepdims=True
@@ -158,13 +182,19 @@
 
         lax.fori_loop(0, order // block, rows_of, 0)
 
-    for index in range(1, pieces):
-        arrivals[index].wait_recv()
-        forward(index)
-    for copy in og_copies:
-        copy.wait_recv()
-    for index in range(pieces):
+    early = pieces - 1
+    for turn in range(max(early, rows)):
+        if turn < rows - 1:
+            wait_hop(turn)
+            if turn + 1 < rows - 1:
+                start_hop(turn + 1)
+        if 1 <= turn + 1 < early:
+            arrivals[turn + 1].wait_recv()
+            forward(turn + 1)
+    for index in range(pieces - 1):
         add_piece(index)
+    arrivals[pieces - 1].wait_recv()
+    add_piece(pieces - 1)
     swap = send(partial.at[:, lanes(1 - side, width)], from_sibling, at_col(0))
 
     diag_copy.wait_recv()
@@ -200,14 +230,15 @@
         w_hi[here, :], w_lo[here, :] = split(rest)
         return carry
 
-    lax.fori_loop(0, order // block, square_rows, 0)
-
+    lax.fori_loop(0, half // block, square_rows, 0)
     swap.wait_recv()
     tile = (partial[:, own_columns] + from_sibling[...]).astype(BF16)
     pair_own[:, own_columns] = tile
     tile_sibling = send(pair_own.at[:, own_columns], pair_own.at[:, own_columns], at_col(0))
     tile_far = send(pair_own.at[:, own_columns], pair_other.at[:, own_columns], at_col(1))
 
+    lax.fori_loop(half // block, order // block, square_rows, 0)
+
     def fourth_rows(step, carry):
         here = lanes(step, block)
         p_hi[here, :], p_lo[here, :] = split(triple(q_hi, q_lo, q_hi, q_lo, here))
@@ -215,49 +246,77 @@
 
     lax.fori_loop(0, half // block, fourth_rows, 0)
 
-    def root_rows(step, carry):
-        here = lanes(step, block)
+    blocks = half // block
+    to_sibling, to_far, handed = [], [], []
+    for step in range(blocks):
+        here = pl.ds(step * block, block)
         value = 5.0 * (f_hi[here, :].astype(F32) + f_lo[here, :].astype(F32))
         value = (value - triple(p_hi, p_lo, w_hi, w_lo, here)) / 4.0
         root[here, :] = value.astype(BF16)
-        return carry
-
-    lax.fori_loop(0, half // block, root_rows, 0)
-    root_copy = send(root, root_sibling, at_col(0))
+        quarter = left_other.at[here, :]
+        to_sibling.append(remote(root.at[here, :], root_sibling.at[here, :], at_col(0)))
+        to_far.append(remote(root.at[here, pl.ds(0, half)], quarter, at_col(1)))
+        handed.append(remote(quarter, quarter, at_col(0)))
+
+        if step == 0:
+            to_sibling[step].start()
+        else:
+            pl.when(side == 0)(to_sibling[step].start)
+        pl.when(side == 0)(to_far[step].start)
+
+    fresh = (1.0 - DECAY) / order
+
+    def gram_part(pair, position, first):
+        def left_rows(step, carry):
+            there = pl.ds(pl.multiple_of(half_index * half + step * block, block), block)
+            here = lanes(step, block)
+            gram = fresh * product(pair[there, :], pair[...], ((1,), (1,)))
+            if first:
+                renewed[here, :] = DECAY * stat[here, :] + gram
+            else:
+                renewed[here, :] += gram
+            return carry
+
+        def right_rows(step, carry):
+            here = lanes(step, block)
+            there = lanes(position, half)
+            gram = product(pair_own[:, here], pair[...], ((0,), (0,)))
+            renewed[here, there] = DECAY * stat[here, there] + fresh * gram
+            return carry
+
+        @pl.when(side == 0)
+        def _():
+            lax.fori_loop(0, blocks, left_rows, 0)
+
+        @pl.when(side == 1)
+        def _():
+            lax.fori_loop(0, blocks, right_rows, 0)
+
+    tile_sibling.wait_recv()
+    gram_part(pair_own, half_index, True)
     tile_far.wait_recv()
     far_sibling = send(pair_other.at[:, own_columns], pair_other.at[:, own_columns], at_col(0))
-    root_copy.wait_recv()
-    left[...] = jnp.where(side == 0, root[...], root_sibling[...])
-    left_copy = send(left.at[:, pl.ds(0, half)], left_other, at_col(1))
-    tile_sibling.wait_recv()
-    far_sibling.wait_recv()
-
-    fresh = (1.0 - DECAY) / order
+    for step in range(blocks):
+        if step == 0:
+            to_sibling[step].wait_recv()
+
+        @pl.when(side == 0)
+        def _():
+            to_far[step].wait_recv()
+            handed[step].start()
 
     @pl.when(side == 0)
     def _():
-        def gram_rows(step, carry):
-            there = pl.ds(pl.multiple_of(half_index * half + step * block, block), block)
-            here = lanes(step, block)
-            gram = product(pair_own[there, :], pair_own[...], ((1,), (1,)))
-            gram += product(pair_other[there, :], pair_other[...], ((1,), (1,)))
-            renewed[here, :] = DECAY * stat[here, :] + fresh * gram
-            return carry
-
-        lax.fori_loop(0, half // block, gram_rows, 0)
+        left[...] = root[...]
 
     @pl.when(side == 1)
     def _():
-        def gram_rows(step, carry):
-            here = lanes(step, block)
-            mine = pair_own[:, here]
-            for position, pair in ((half_index, pair_own), (1 - half_index, pair_other)):
-                there = lanes(position, half)
-                gram = product(mine, pair[...], ((0,), (0,)))
-                renewed[here, there] = DECAY * stat[here, there] + fresh * gram
-            return carry
-
-        lax.fori_loop(0, half // block, gram_rows, 0)
+        for copy in to_sibling[1:]:
+            copy.wait_recv()
+        left[...] = root_sibling[...]
+
+    far_sibling.wait_recv()
+    gram_part(pair_other, 1 - half_index, False)
 
     right = jnp.where(side == 0, root_sibling[:width, :], root[half - width :, :])
     for place, natural in ((0, half_index), (1, 1 - half_index)):
@@ -267,7 +326,12 @@
         hp[place * half : (place + 1) * half, :] = value.astype(BF16)
     cond_own = product(left[...], hp[...])
     cond_other = product(left[:, half:], hp[:half, :], ((0,), (0,)))
-    left_copy.wait_recv()
+
+    @pl.when(side == 1)
+    def _():
+        for copy in handed:
+            copy.wait_recv()
+
     cond_other += product(left_other[...], hp[half:, :])
     values = pair_own[:, own_columns].astype(F32)
     count = order * width
@@ -276,10 +340,16 @@
     update[lanes(half_index, half), :] = (cond_own * ratio).astype(BF16)
     update[lanes(1 - half_index, half), :] = (cond_other * ratio).astype(BF16)
 
-    everything = [list(arrivals.values()), og_copies]
-    everything += [[diag_copy, swap, tile_sibling, tile_far, root_copy, far_sibling, left_copy]]
-    for group in everything:
-        for copy in group:
+    everything = list(arrivals.values())
+    everything += [diag_copy, swap, tile_sibling, tile_far, far_sibling, to_sibling[0]]
+    for copy in everything:
+        copy.wait_send()
+    for _, copy, sends, _ in hops:
+        pl.when(sends)(copy.wait_send)
+
+    @pl.when(side == 0)
+    def _():
+        for copy in to_sibling[1:] + to_far + handed:
             copy.wait_send()
 
 
@@ -289,7 +359,7 @@
     piece = activations.shape[0]
     width = out_grads.shape[1]
     pieces = cols // 2
-    copies = pieces - 1 + rows - 1 + 8
+    copies = pieces - 1 + 2 * (rows - 1) + 6 + 3 * (half // width)
     square = pltpu.VMEM((order, order), BF16)
     strip = pltpu.VMEM((half, order), BF16)
     pair = pltpu.VMEM((order, 2 * width), BF16)

time: 101 us -> 89.2 us (0.88)
  Pallas kernels: 95.4 us -> 84.3 us
    pallas_call x1, Pallas kernels: 95.4 us -> 84.3 us  [local(): pl.pallas_call(functools.partial(shampoo_kernel, rows, cols), out_shape=(...]
where the time goes in v1:
time: 89.2 us; the launch traced here: 89 us
  Pallas kernels  84.3 us (95%)
  local copies, waits for them, and re-layouts  4.01 us (4%)
    pallas_call x1, Pallas kernels, local(): pl.pallas_call(functools.partial(shampoo_kernel, rows, cols), out_shape=(...  84.3 us
    unnamed x4, local copies, waits for them, and re-layouts  4.01 us

profile of v1, /device:TPU:0, one launch (start us, length us, event | category | flops | bytes accessed | tf_op | source)
XLA Modules:
  0.0 89.0 jit_solution(11212634439137179841)
XLA Ops:
  0.6 84.3 %shard_map.50 = (f32[512,1024]{1,0:T(8,128)}, bf16[1024,256]{1,0:T(8,128)(2,1)}) custom-call(bf16[512,1024]{1,0:T(8,128)(2,1)} %act.1, bf16[1024,256]{1,0:T(8,128)(2,1)} %og.1, f32[512,1024]{1,0:T(8,128)} %bitcast.2), custom_call_target="tpu_custom_call" | custom-call | tf_op jit(solution)/shard_map/pallas_call | solution.py:366
  85.0 0.0 copy-start
  85.0 3.2 %copy.7 = f32[1,1,512,1024]{3,2,1,0:T(8,128)} copy(f32[1,1,512,1024]{3,2,1,0:T(8,128)} %bitcast.3) | data formatting | bytes 4194304
  88.2 0.0 copy-done
  88.2 0.8 copy.8
Async XLA Ops:
  85.0 3.2 %copy-start = (bf16[1024,256]{1,0:T(8,128)(2,1)S(1)}, bf16[1024,256]{1,0:T(8,128)(2,1)}, u32[]{:S(2)}) copy-start(bf16[1024,256]{1,0:T(8,128)(2,1)} %get-tuple-element.9) | copy-start | bytes 1572868

commit v2 on v1

--- a/solution.py
+++ b/solution.py
@@ -60,6 +60,9 @@
     left,
     left_other,
     hp,
+    facts,
+    far_facts,
+    squares,
     send_sem,
     recv_sem,
     local_sem,
@@ -128,7 +131,6 @@
     )
     kept.start()
     forward(0)
-    diag_copy = send(stat.at[:, lanes(half_index, half)], other_diag, at_col(1))
     kept.wait()
     sibling_og.wait()
 
@@ -164,8 +166,13 @@
         == lax.broadcasted_iota(jnp.int32, (half, half), 1)
     ).astype(F32)
     own_trace = total(stat[:, lanes(half_index, half)] * eye)
-
-    def add_piece(index):
+    facts[0:1, :] = jnp.broadcast_to(own_max, (1, 128))
+    facts[1:2, :] = jnp.broadcast_to(own_trace, (1, 128))
+    facts[2:8, :] = jnp.zeros((6, 128), F32)
+    facts_copy = send(facts, far_facts, at_col(1))
+    diag_copy = send(stat.at[:, lanes(half_index, half)], other_diag, at_col(1))
+
+    def add_piece(index, first, last):
         source = col // 2
         for bit in range(bits):
             if index >> bit & 1:
@@ -180,7 +187,35 @@
                 partial[here, :] += term
             return carry
 
-        lax.fori_loop(0, order // block, rows_of, 0)
+        lax.fori_loop(first, last, rows_of, 0)
+
+    def triple(a_hi, a_lo, b_hi, b_lo, here, along=slice(None)):
+        return (
+            product(a_hi[here, along], b_hi[along, :])
+            + product(a_hi[here, along], b_lo[along, :])
+            + product(a_lo[here, along], b_hi[along, :])
+        )
+
+    def prepare():
+        facts_copy.wait_recv()
+        trace = own_trace + far_facts[1:2, 0:1]
+        damping = 10.0 ** (-DAMP_EXP) * trace / order
+        scaling = (jnp.maximum(own_max, far_facts[0:1, 0:1]) + damping) / 4.0
+        scale = 0.25 / scaling
+        shift = 1.25 - damping * scale
+        top = shift * eye - stat[:, lanes(half_index, half)] * scale
+        f_hi[:half, :half], f_lo[:half, :half] = split(top)
+        off = -(stat[:, lanes(1 - half_index, half)] * scale)
+        f_hi[:half, half:], f_lo[:half, half:] = split(off)
+        f_hi[half:, :half], f_lo[half:, :half] = split(off.T)
+
+        def near_rows(step, carry):
+            here = lanes(step, block)
+            squares[here, :] = triple(f_hi, f_lo, f_hi, f_lo, here, slice(0, half))
+            return carry
+
+        lax.fori_loop(0, order // block, near_rows, 0)
+        return scale, shift
 
     early = pieces - 1
     for turn in range(max(early, rows)):
@@ -191,53 +226,47 @@
         if 1 <= turn + 1 < early:
             arrivals[turn + 1].wait_recv()
             forward(turn + 1)
+        if turn == 1:
+            scale, shift = prepare()
     for index in range(pieces - 1):
-        add_piece(index)
+        add_piece(index, 0, order // block)
     arrivals[pieces - 1].wait_recv()
-    add_piece(pieces - 1)
-    swap = send(partial.at[:, lanes(1 - side, width)], from_sibling, at_col(0))
+    blocks = half // block
+    swaps = []
+    for chunk in range(2):
+        add_piece(pieces - 1, chunk * blocks, (chunk + 1) * blocks)
+        strip = pl.ds(chunk * half, half)
+        swaps.append(
+            send(
+                partial.at[strip, lanes(1 - side, width)], from_sibling.at[strip, :], at_col(0)
+            )
+        )
 
     diag_copy.wait_recv()
-    own_off = stat[:, lanes(1 - half_index, half)]
-    far = other_diag[...]
-    far_sums = jnp.sum(jnp.abs(own_off), axis=0, keepdims=True) + jnp.sum(
-        jnp.abs(far), axis=0, keepdims=True
-    )
-    far_max = jnp.max(far_sums, axis=1, keepdims=True)
-    damping = 10.0 ** (-DAMP_EXP) * (own_trace + total(far * eye)) / order
-    scaling = (jnp.maximum(own_max, far_max) + damping) / 4.0
-    scale = 0.25 / scaling
-    shift = 1.25 - damping * scale
-    top = shift * eye - stat[:, lanes(half_index, half)] * scale
-    f_hi[:half, :half], f_lo[:half, :half] = split(top)
-    off = -(own_off * scale)
-    f_hi[:half, half:], f_lo[:half, half:] = split(off)
-    f_hi[half:, :half], f_lo[half:, :half] = split(off.T)
-    f_hi[half:, half:], f_lo[half:, half:] = split(shift * eye - far * scale)
-
-    def triple(a_hi, a_lo, b_hi, b_lo, here):
-        return (
-            product(a_hi[here, :], b_hi[...])
-            + product(a_hi[here, :], b_lo[...])
-            + product(a_lo[here, :], b_hi[...])
-        )
+    f_hi[half:, half:], f_lo[half:, half:] = split(shift * eye - other_diag[...] * scale)
 
     def square_rows(step, carry):
         here = lanes(step, block)
-        square = triple(f_hi, f_lo, f_hi, f_lo, here)
+        square = squares[here, :]
+        square += triple(f_hi, f_lo, f_hi, f_lo, here, slice(half, order))
         q_hi[here, :], q_lo[here, :] = split(square)
         rest = 5.0 * (f_hi[here, :].astype(F32) + f_lo[here, :].astype(F32)) - 4.0 * square
         w_hi[here, :], w_lo[here, :] = split(rest)
         return carry
 
-    lax.fori_loop(0, half // block, square_rows, 0)
-    swap.wait_recv()
-    tile = (partial[:, own_columns] + from_sibling[...]).astype(BF16)
-    pair_own[:, own_columns] = tile
-    tile_sibling = send(pair_own.at[:, own_columns], pair_own.at[:, own_columns], at_col(0))
-    tile_far = send(pair_own.at[:, own_columns], pair_other.at[:, own_columns], at_col(1))
-
-    lax.fori_loop(half // block, order // block, square_rows, 0)
+    tile_sibling, tile_far, far_sibling = [], [], []
+    for chunk in range(2):
+        lax.fori_loop(chunk, chunk + 1, square_rows, 0)
+        strip = pl.ds(chunk * half, half)
+        swaps[chunk].wait_recv()
+        tile = (partial[strip, own_columns] + from_sibling[strip, :]).astype(BF16)
+        pair_own[strip, own_columns] = tile
+        mine = pair_own.at[strip, own_columns]
+        there = pair_other.at[strip, own_columns]
+        tile_far.append(send(mine, there, at_col(1)))
+        tile_sibling.append(send(mine, mine, at_col(0)))
+        far_sibling.append(remote(there, there, at_col(0)))
+    lax.fori_loop(2, order // block, square_rows, 0)
 
     def fourth_rows(step, carry):
         here = lanes(step, block)
@@ -246,7 +275,6 @@
 
     lax.fori_loop(0, half // block, fourth_rows, 0)
 
-    blocks = half // block
     to_sibling, to_far, handed = [], [], []
     for step in range(blocks):
         here = pl.ds(step * block, block)
@@ -292,10 +320,13 @@
         def _():
             lax.fori_loop(0, blocks, right_rows, 0)
 
-    tile_sibling.wait_recv()
+    tile_far[0].wait_recv()
+    far_sibling[0].start()
+    for copy in tile_sibling:
+        copy.wait_recv()
     gram_part(pair_own, half_index, True)
-    tile_far.wait_recv()
-    far_sibling = send(pair_other.at[:, own_columns], pair_other.at[:, own_columns], at_col(0))
+    tile_far[1].wait_recv()
+    far_sibling[1].start()
     for step in range(blocks):
         if step == 0:
             to_sibling[step].wait_recv()
@@ -315,7 +346,8 @@
             copy.wait_recv()
         left[...] = root_sibling[...]
 
-    far_sibling.wait_recv()
+    for copy in far_sibling:
+        copy.wait_recv()
     gram_part(pair_other, 1 - half_index, False)
 
     right = jnp.where(side == 0, root_sibling[:width, :], root[half - width :, :])
@@ -341,7 +373,8 @@
     update[lanes(1 - half_index, half), :] = (cond_other * ratio).astype(BF16)
 
     everything = list(arrivals.values())
-    everything += [diag_copy, swap, tile_sibling, tile_far, far_sibling, to_sibling[0]]
+    everything += swaps + tile_sibling + tile_far + far_sibling
+    everything += [diag_copy, facts_copy, to_sibling[0]]
     for copy in everything:
         copy.wait_send()
     for _, copy, sends, _ in hops:
@@ -359,7 +392,7 @@
     piece = activations.shape[0]
     width = out_grads.shape[1]
     pieces = cols // 2
-    copies = pieces - 1 + 2 * (rows - 1) + 6 + 3 * (half // width)
+    copies = pieces - 1 + 2 * (rows - 1) + 11 + 3 * (half // width)
     square = pltpu.VMEM((order, order), BF16)
     strip = pltpu.VMEM((half, order), BF16)
     pair = pltpu.VMEM((order, 2 * width), BF16)
@@ -392,6 +425,9 @@
             strip,
             pltpu.VMEM((half, half), BF16),
             pltpu.VMEM((order, width), BF16),
+            pltpu.VMEM((8, 128), F32),
+            pltpu.VMEM((8, 128), F32),
+            pltpu.VMEM((order, order), F32),
             pltpu.SemaphoreType.DMA((copies,)),
             pltpu.SemaphoreType.DMA((copies,)),
             pltpu.SemaphoreType.DMA((1,)),

time: 89.2 us -> 86.3 us (0.967)
  Pallas kernels: 84.3 us -> 81.5 us
    pallas_call x1, Pallas kernels: 84.3 us -> 81.5 us  [local(): pl.pallas_call(functools.partial(shampoo_kernel, rows, cols), out_shape=(...]
where the time goes in v2:
time: 86.3 us; the launch traced here: 86.2 us
  Pallas kernels  81.5 us (94%)
  local copies, waits for them, and re-layouts  4.01 us (5%)
    pallas_call x1, Pallas kernels, local(): pl.pallas_call(functools.partial(shampoo_kernel, rows, cols), out_shape=(...  81.5 us
    unnamed x4, local copies, waits for them, and re-layouts  4.01 us

profile of v2, /device:TPU:0, one launch (start us, length us, event | category | flops | bytes accessed | tf_op | source)
XLA Modules:
  0.0 86.2 jit_solution(1815622112696176996)
XLA Ops:
  0.6 81.5 %shard_map.50 = (f32[512,1024]{1,0:T(8,128)}, bf16[1024,256]{1,0:T(8,128)(2,1)}) custom-call(bf16[512,1024]{1,0:T(8,128)(2,1)} %act.1, bf16[1024,256]{1,0:T(8,128)(2,1)} %og.1, f32[512,1024]{1,0:T(8,128)} %bitcast.2), custom_call_target="tpu_custom_call" | custom-call | tf_op jit(solution)/shard_map/pallas_call | solution.py:399
  82.2 0.0 copy-start
  82.2 3.2 %copy.7 = f32[1,1,512,1024]{3,2,1,0:T(8,128)} copy(f32[1,1,512,1024]{3,2,1,0:T(8,128)} %bitcast.3) | data formatting | bytes 4194304
  85.4 0.0 copy-done
  85.4 0.8 copy.8
Async XLA Ops:
  82.2 3.2 %copy-start = (bf16[1024,256]{1,0:T(8,128)(2,1)S(1)}, bf16[1024,256]{1,0:T(8,128)(2,1)}, u32[]{:S(2)}) copy-start(bf16[1024,256]{1,0:T(8,128)(2,1)} %get-tuple-element.9) | copy-start | bytes 1572868

commit v3 on v2

--- a/solution.py
+++ b/solution.py
@@ -433,7 +433,7 @@
             pltpu.SemaphoreType.DMA((1,)),
         ],
         compiler_params=pltpu.CompilerParams(
-            collective_id=0, has_side_effects=True, vmem_limit_bytes=60 * 1024 * 1024
+            collective_id=0, has_side_effects=True, vmem_limit_bytes=48 * 1024 * 1024
         ),
     )(activations, out_grads, stat)
     return (renewed[None, None], update)

time: 86.3 us -> 84.8 us (0.983)
  Pallas kernels: 81.5 us -> 79.5 us
    pallas_call x1, Pallas kernels: 81.5 us -> 79.5 us  [local(): pl.pallas_call(functools.partial(shampoo_kernel, rows, cols), out_shape=(...]
    unnamed x4 -> x6, local copies, waits for them, and re-layouts: 4.01 us -> 4.37 us
where the time goes in v3:
time: 84.8 us; the launch traced here: 84.5 us
  Pallas kernels  79.5 us (94%)
  local copies, waits for them, and re-layouts  4.37 us (5%)
    pallas_call x1, Pallas kernels, local(): pl.pallas_call(functools.partial(shampoo_kernel, rows, cols), out_shape=(...  79.5 us
    unnamed x6, local copies, waits for them, and re-layouts  4.37 us

profile of v3, /device:TPU:0, one launch (start us, length us, event | category | flops | bytes accessed | tf_op | source)
XLA Modules:
  0.0 84.5 jit_solution(13698414799361774180)
XLA Ops:
  0.6 0.0 copy-start
  0.6 1.2 %copy-done = bf16[512,1024]{1,0:T(8,128)(2,1)S(1)} copy-done((bf16[512,1024]{1,0:T(8,128)(2,1)S(1)}, bf16[512,1024]{1,0:T(8,128)(2,1)}, u32[]{:S(2)}) %copy-start) | copy-done | bytes 1048600
  1.9 0.0 copy-start.1
  1.9 1.0 %copy-done.1 = bf16[1024,256]{1,0:T(8,128)(2,1)S(1)} copy-done((bf16[1024,256]{1,0:T(8,128)(2,1)S(1)}, bf16[1024,256]{1,0:T(8,128)(2,1)}, u32[]{:S(2)}) %copy-start.1) | copy-done | bytes 524312
  2.9 79.5 %shard_map.50 = (f32[512,1024]{1,0:T(8,128)S(1)}, bf16[1024,256]{1,0:T(8,128)(2,1)S(1)}) custom-call(bf16[512,1024]{1,0:T(8,128)(2,1)S(1)} %copy-done, bf16[1024,256]{1,0:T(8,128)(2,1)S(1)} %copy-done.1, f32[512,1024]{1,0:T(8,128)} %bitcast.3), custom_call_target="tpu_custom_call" | custom-call | tf_op jit(solution)/shard_map/pallas_call | solution.py:399
  82.4 1.3 %copy.7 = f32[1,1,512,1024]{3,2,1,0:T(8,128)} copy(f32[1,1,512,1024]{3,2,1,0:T(8,128)S(1)} %bitcast.2) | data formatting | bytes 4194304
  83.7 0.8 copy.8
Async XLA Ops:
  0.6 1.2 %copy-start = (bf16[512,1024]{1,0:T(8,128)(2,1)S(1)}, bf16[512,1024]{1,0:T(8,128)(2,1)}, u32[]{:S(2)}) copy-start(bf16[512,1024]{1,0:T(8,128)(2,1)} %act.1) | copy-start | bytes 3145732
  1.9 1.0 %copy-start.1 = (bf16[1024,256]{1,0:T(8,128)(2,1)S(1)}, bf16[1024,256]{1,0:T(8,128)(2,1)}, u32[]{:S(2)}) copy-start(bf16[1024,256]{1,0:T(8,128)(2,1)} %og.1) | copy-start | bytes 1572868
